TPU v7x, 512 devices: a whole 4x8x8 slice. The times are simulated.
512 devices in a mesh: src: 16 (over y, x_hi), space: 32 (over x_lo, z, core).
Axes of the slice: x: 4 (x_hi: 2, x_lo: 2; x = x_hi * 2 + x_lo), y: 8, z: 8, core: 2. Of those that a mesh axis runs over, the one named last changes fastest.
Arguments:
- velocity: float32 [32, 512, 256], P('space'), may hold values from 0.5 to 2
- station_cells: int32 [16, 3], P('src'), may hold values from 0 to 511, as said below
- event_cells: int32 [3, 8192], replicated, may hold values from 0 to 511, as said below
- delays: float32 [16, 8192], P('src'), may hold values from -6 to 6
- active: int32 [2, 16, 32, 16], P(None, 'src', 'space'), may hold values from 0 to 1, as said below
Outputs:
- traveltimes: float32 [16, 32, 512, 256], P('src', 'space')
- kernel: float32 [32, 512, 256], P('space', 'src')
Inputs may be any that keep to these rules, and one draw needn't show every extreme that they name: `station_cells`: stations lie in the top four layers: third coordinate below 4, first below 32, second below 512. `event_cells`: row 0 holds first coordinates below 32, row 1 second ones below 512, row 2 third ones below 256. `active`: 1 marks a tile whose cells are updated in that round for that station.
All inputs are finite; a program needn't handle non-finite values.
Results may differ from a plain program's by a relative error of at most 0.0003.
Values sent between devices are 32-bit elements; how exact they have to be, the bound alone decides.
A program may use at most 64 MiB of HBM per device.

v0:
```python
import jax
import jax.numpy as jnp
from jax import lax
from jax.sharding import PartitionSpec as P

TY = 32
ROUNDS = 2
SWEEPS = 2
ADJ_SWEEPS = 4
BIG = 1000000.0


def padded(array, sides, width):
    for axis, dim in sides:
        size, length = (lax.axis_size(axis), array.shape[dim])
        up = [(i, (i + 1) % size) for i in range(size - 1)]
        down = [(j, i) for i, j in up]
        last = lax.slice_in_dim(array, length - width, length, axis=dim)
        first = lax.slice_in_dim(array, 0, width, axis=dim)
        before = lax.ppermute(last, axis, up)
        after = lax.ppermute(first, axis, down)
        array = jnp.concatenate([before, array, after], axis=dim)
    return array


def godunov(near_x, near_y, near_z, cost_cell):
    lowest = jnp.minimum(jnp.minimum(near_x, near_y), near_z)
    highest = jnp.maximum(jnp.maximum(near_x, near_y), near_z)
    middle = jnp.maximum(
        jnp.minimum(near_x, near_y), jnp.minimum(jnp.maximum(near_x, near_y), near_z)
    )
    first_gap = middle - lowest
    second_gap = highest - lowest
    single = lowest + cost_cell
    double = lowest + 0.5 * (
        first_gap + jnp.sqrt(jnp.maximum(2.0 * cost_cell * cost_cell - first_gap * first_gap, 0.0))
    )
    gaps = first_gap + second_gap
    triple = (
        lowest
        + (
            gaps
            + jnp.sqrt(
                jnp.maximum(
                    gaps * gaps
                    - 3.0
                    * (first_gap * first_gap + second_gap * second_gap - cost_cell * cost_cell),
                    0.0,
                )
            )
        )
        / 3.0
    )
    return jnp.where(single <= middle, single, jnp.where(double <= highest, double, triple))


def end_slab(field, axis_index, fill):
    return jnp.full_like(lax.slice_in_dim(field, 0, 1, axis=axis_index), fill)


def shifted(field, axis_index, low_rim, high_rim):
    length = field.shape[axis_index]
    before = jnp.concatenate(
        [low_rim, lax.slice_in_dim(field, 0, length - 1, axis=axis_index)], axis=axis_index
    )
    after = jnp.concatenate(
        [lax.slice_in_dim(field, 1, length, axis=axis_index), high_rim], axis=axis_index
    )
    return (before, after)


def six_neighbours(field, low_rim, high_rim, fill):
    x_before, x_after = shifted(field, 1, low_rim, high_rim)
    y_before, y_after = shifted(field, 2, end_slab(field, 2, fill), end_slab(field, 2, fill))
    z_before, z_after = shifted(field, 3, end_slab(field, 3, fill), end_slab(field, 3, fill))
    return [x_before, x_after, y_before, y_after, z_before, z_after]


def outer_rims(extended):
    position = lax.axis_index("space")
    final_index = lax.axis_size("space") - 1
    low_rim = jnp.where(position == 0, BIG, extended[:, :1])
    high_rim = jnp.where(position == final_index, BIG, extended[:, -1:])
    return (low_rim, high_rim)


def sweep_once(times, slowness, tile_mask, station_mask):
    extended = padded(times, (("space", 1),), 1)
    low_rim, high_rim = outer_rims(extended)
    beside_all = six_neighbours(times, low_rim, high_rim, BIG)
    update = godunov(
        jnp.minimum(beside_all[0], beside_all[1]),
        jnp.minimum(beside_all[2], beside_all[3]),
        jnp.minimum(beside_all[4], beside_all[5]),
        slowness[None],
    )
    station_count, rows_x, rows_y, rows_z = times.shape
    tile_count = rows_y // TY
    shape_tiles = (station_count, rows_x, tile_count, TY, rows_z)
    chosen = jnp.where(tile_mask, update.reshape(shape_tiles), times.reshape(shape_tiles)).reshape(
        times.shape
    )
    return jnp.where(station_mask, 0.0, chosen)


def smooth_along(extended, axis_index):
    length = extended.shape[axis_index]
    first = lax.slice_in_dim(extended, 0, length - 2, axis=axis_index)
    centre = lax.slice_in_dim(extended, 1, length - 1, axis=axis_index)
    after = lax.slice_in_dim(extended, 2, length, axis=axis_index)
    return (first + 2.0 * centre + after) * 0.25


def pad_zero(field, axis_index):
    widths = [(0, 0)] * field.ndim
    widths[axis_index] = (1, 1)
    return jnp.pad(field, widths)


def per_device(velocity, station_cells, event_cells, delays, active):
    slowness = 1.0 / velocity
    rows_x, rows_y, rows_z = velocity.shape
    station_count = station_cells.shape[0]
    offset_x = lax.axis_index("space") * rows_x
    grid_x = (lax.broadcasted_iota(jnp.int32, (rows_x, rows_y, rows_z), 0) + offset_x)[None]
    grid_y = lax.broadcasted_iota(jnp.int32, (rows_x, rows_y, rows_z), 1)[None]
    grid_z = lax.broadcasted_iota(jnp.int32, (rows_x, rows_y, rows_z), 2)[None]
    station_x = station_cells[:, 0][:, None, None, None]
    station_y = station_cells[:, 1][:, None, None, None]
    station_z = station_cells[:, 2][:, None, None, None]
    diff_x = (grid_x - station_x).astype(jnp.float32)
    diff_y = (grid_y - station_y).astype(jnp.float32)
    diff_z = (grid_z - station_z).astype(jnp.float32)
    times = jnp.sqrt(diff_x * diff_x + diff_y * diff_y + diff_z * diff_z)
    station_mask = (grid_x == station_x) & (grid_y == station_y) & (grid_z == station_z)
    for round_index in range(ROUNDS):
        tile_mask = (active[round_index][:, 0, :] > 0)[:, None, :, None, None]
        for sweep in range(SWEEPS):
            times = sweep_once(times, slowness, tile_mask, station_mask)
    cell_count = rows_x * rows_y * rows_z
    event_x = event_cells[0]
    event_y = event_cells[1]
    event_z = event_cells[2]
    local_x = event_x - offset_x
    inside = (local_x >= 0) & (local_x < rows_x)
    flat_index = jnp.where(
        inside, local_x * (rows_y * rows_z) + event_y * rows_z + event_z, cell_count
    )
    flat_times = times.reshape(station_count, cell_count)
    picked = jnp.take(flat_times, jnp.minimum(flat_index, cell_count - 1), axis=1)
    event_dx = (event_x[None, :] - station_cells[:, 0:1]).astype(jnp.float32)
    event_dy = (event_y[None, :] - station_cells[:, 1:2]).astype(jnp.float32)
    event_dz = (event_z[None, :] - station_cells[:, 2:3]).astype(jnp.float32)
    direct = jnp.sqrt(event_dx * event_dx + event_dy * event_dy + event_dz * event_dz)
    misfit = jnp.where(inside[None, :], picked - direct - delays, 0.0)
    source = (
        jnp.zeros((station_count, cell_count), jnp.float32)
        .at[:, flat_index]
        .add(misfit, mode="drop")
    )
    source = source.reshape(times.shape)
    final_ext = padded(times, (("space", 1),), 1)
    low_rim, high_rim = outer_rims(final_ext)
    time_around = six_neighbours(times, low_rim, high_rim, BIG)
    weights = [
        jnp.maximum(neighbour - times, 0.0) * velocity[None] / 6.0 for neighbour in time_around
    ]
    adjoint = source
    for sweep in range(ADJ_SWEEPS):
        adjoint_ext = padded(adjoint, (("space", 1),), 1)
        adjoint_around = six_neighbours(adjoint, adjoint_ext[:, :1], adjoint_ext[:, -1:], 0.0)
        summed = source
        for weight, neighbour in zip(weights, adjoint_around):
            summed = summed + weight * neighbour
        adjoint = summed
    density = slowness * jnp.sum(adjoint, axis=0)
    summed_density = lax.psum(density, "src")
    extended = padded(summed_density, (("space", 0),), 1)
    along_x = smooth_along(extended, 0)
    along_y = smooth_along(pad_zero(along_x, 1), 1)
    filtered = smooth_along(pad_zero(along_y, 2), 2)
    row_count = rows_y // lax.axis_size("src")
    kernel = lax.dynamic_slice_in_dim(filtered, lax.axis_index("src") * row_count, row_count, 1)
    return (times, kernel)


def solution(mesh):
    return jax.shard_map(
        per_device,
        mesh=mesh,
        in_specs=(
            P("space", None, None),
            P("src", None),
            P(),
            P("src", None),
            P(None, "src", "space", None),
        ),
        out_specs=(P("src", "space", None, None), P("space", "src", None)),
        check_vma=False,
    )
```

profile of v0, /device:TPU:2, one launch (start us, length us, event | category | flops | bytes accessed | tf_op | source)
XLA Modules:
  0.0 430.9 jit_solution(12294616544357058122)
XLA Ops:
  10.4 10.4 %collective-permute-start.1 = (f32[1,1,512,256]{3,2,1,0:T(8,128)S(1)}, f32[1,1,512,256]{3,2,1,0:T(8,128)S(1)}, u32[]{:S(2)}, u32[]{:S(2)}) collective-permute-start(f32[1,1,512,256]{3,2,1,0:T(8,128)S(1)} %add_sqrt_fusion), channel_id=1, source_target_pairs={{1,0},{2,1},{3,2},{4,3},{5,4},{6,5},{7,6},{8,7},{9,8},{10,9},{11,1... | collective-permute-start | bytes 1572872 | tf_op jit(solution)/shard_map/ppermute | solution.py:21
  27.5 5.9 %collective-permute-done = f32[1,1,512,256]{3,2,1,0:T(8,128)S(1)} collective-permute-done((f32[1,1,512,256]{3,2,1,0:T(8,128)S(1)}, f32[1,1,512,256]{3,2,1,0:T(8,128)S(1)}, u32[]{:S(2)}, u32[]{:S(2)}) %collective-permute-start) | collective-permute-done | bytes 524320 | tf_op jit(solution)/shard_map/ppermute | solution.py:20
  33.4 2.6 fusion.1
  37.9 2.4 collective-permute-start.2
  40.6 4.0 collective-permute-done.3
  44.6 5.9 %collective-permute-done.2 = f32[1,1,512,256]{3,2,1,0:T(8,128)S(1)} collective-permute-done((f32[1,1,512,256]{3,2,1,0:T(8,128)S(1)}, f32[1,1,512,256]{3,2,1,0:T(8,128)S(1)}, u32[]{:S(2)}, u32[]{:S(2)}) %collective-permute-start.2) | collective-permute-done | bytes 524320 | tf_op jit(solution)/shard_map/ppermute | solution.py:20
  54.7 2.4 collective-permute-start.4
  57.4 4.0 collective-permute-done.5
  61.4 5.9 %collective-permute-done.4 = f32[1,1,512,256]{3,2,1,0:T(8,128)S(1)} collective-permute-done((f32[1,1,512,256]{3,2,1,0:T(8,128)S(1)}, f32[1,1,512,256]{3,2,1,0:T(8,128)S(1)}, u32[]{:S(2)}, u32[]{:S(2)}) %collective-permute-start.4) | collective-permute-done | bytes 524320 | tf_op jit(solution)/shard_map/ppermute | solution.py:20
  71.5 2.4 collective-permute-start.6
  74.2 4.0 collective-permute-done.7
  78.2 5.9 %collective-permute-done.6 = f32[1,1,512,256]{3,2,1,0:T(8,128)S(1)} collective-permute-done((f32[1,1,512,256]{3,2,1,0:T(8,128)S(1)}, f32[1,1,512,256]{3,2,1,0:T(8,128)S(1)}, u32[]{:S(2)}, u32[]{:S(2)}) %collective-permute-start.6) | collective-permute-done | bytes 524320 | tf_op jit(solution)/shard_map/ppermute | solution.py:20
  84.1 2.3 fusion.7
  86.7 45.5 %gather_fusion = f32[8192]{0:T(1024)S(1)} fusion(f32[131072]{0:T(1024)S(1)} %bitcast.79, s32[8192]{0:T(1024)S(1)} %broadcast_clamp_fusion), kind=kCustom, calls=%fused_computation | custom fusion | bytes 98304 | tf_op jit(solution)/shard_map/jit(_take)/gather | solution.py:150
  134.3 43.3 %scatter_custom_fusion = f32[131072]{0:T(1024)S(1)} fusion(s32[8192]{0:T(1024)S(1)} %bitcast.84, f32[8192]{0:T(1024)S(1)} %bitcast.83, f32[]{:T(128)} %constant.24.clone.1), kind=kCustom, calls=%fused_computation.66 | custom fusion | flops 8192 | bytes 524292 | tf_op jit(solution)/shard_map/scatter-add | solution.py:159
  179.8 2.4 collective-permute-start.9
  182.2 5.3 %collective-permute-start.10 = (f32[1,1,512,256]{3,2,1,0:T(8,128)S(1)}, f32[1,1,512,256]{3,2,1,0:T(8,128)S(1)}, u32[]{:S(2)}, u32[]{:S(2)}) collective-permute-start(f32[1,1,512,256]{3,2,1,0:T(8,128)S(1)} %fusion.7), channel_id=1, source_target_pairs={{1,0},{2,1},{3,2},{4,3},{5,4},{6,5},{7,6},{8,7},{9,8},{10,9},{11,1... | collective-permute-start | bytes 1572872 | tf_op jit(solution)/shard_map/ppermute | solution.py:21
  190.1 2.3 collective-permute-done.9
  194.1 5.9 %collective-permute-done.8 = f32[1,1,512,256]{3,2,1,0:T(8,128)S(1)} collective-permute-done((f32[1,1,512,256]{3,2,1,0:T(8,128)S(1)}, f32[1,1,512,256]{3,2,1,0:T(8,128)S(1)}, u32[]{:S(2)}, u32[]{:S(2)}) %collective-permute-start.8) | collective-permute-done | bytes 524320 | tf_op jit(solution)/shard_map/ppermute | solution.py:20
  202.9 2.4 collective-permute-start.12
  205.6 4.0 collective-permute-done.13
  209.6 5.9 %collective-permute-done.12 = f32[1,1,512,256]{3,2,1,0:T(8,128)S(1)} collective-permute-done((f32[1,1,512,256]{3,2,1,0:T(8,128)S(1)}, f32[1,1,512,256]{3,2,1,0:T(8,128)S(1)}, u32[]{:S(2)}, u32[]{:S(2)}) %collective-permute-start.12) | collective-permute-done | bytes 524320 | tf_op jit(solution)/shard_map/ppermute | solution.py:20
  217.9 2.4 collective-permute-start.14
  220.6 4.0 collective-permute-done.15
  224.6 5.9 %collective-permute-done.14 = f32[1,1,512,256]{3,2,1,0:T(8,128)S(1)} collective-permute-done((f32[1,1,512,256]{3,2,1,0:T(8,128)S(1)}, f32[1,1,512,256]{3,2,1,0:T(8,128)S(1)}, u32[]{:S(2)}, u32[]{:S(2)}) %collective-permute-start.14) | collective-permute-done | bytes 524320 | tf_op jit(solution)/shard_map/ppermute | solution.py:20
  232.9 2.4 collective-permute-start.16
  235.6 4.0 collective-permute-done.17
  239.6 5.9 %collective-permute-done.16 = f32[1,1,512,256]{3,2,1,0:T(8,128)S(1)} collective-permute-done((f32[1,1,512,256]{3,2,1,0:T(8,128)S(1)}, f32[1,1,512,256]{3,2,1,0:T(8,128)S(1)}, u32[]{:S(2)}, u32[]{:S(2)}) %collective-permute-start.16) | collective-permute-done | bytes 524320 | tf_op jit(solution)/shard_map/ppermute | solution.py:20
  247.0 159.3 %all-reduce.40.cloned.1.call-done = f32[1,512,256]{2,1,0:T(8,128)} async-done(((f32[1,512,256]{2,1,0:T(8,128)}), f32[1,512,256]{2,1,0:T(8,128)}) %all-reduce.40.cloned.1.call-update) | async-done | bytes 524304 | tf_op jit(solution)/shard_map/psum | solution.py:177
  408.2 2.4 collective-permute-start.18
  410.6 4.6 %collective-permute-done.19 = f32[1,512,256]{2,1,0:T(8,128)S(1)} collective-permute-done((f32[1,512,256]{2,1,0:T(8,128)}, f32[1,512,256]{2,1,0:T(8,128)S(1)}, u32[]{:S(2)}, u32[]{:S(2)}) %collective-permute-start.19) | collective-permute-done | bytes 524320 | tf_op jit(solution)/shard_map/ppermute | solution.py:21
  415.2 6.5 %collective-permute-done.18 = f32[1,512,256]{2,1,0:T(8,128)S(1)} collective-permute-done((f32[1,512,256]{2,1,0:T(8,128)}, f32[1,512,256]{2,1,0:T(8,128)S(1)}, u32[]{:S(2)}, u32[]{:S(2)}) %collective-permute-start.18) | collective-permute-done | bytes 524320 | tf_op jit(solution)/shard_map/ppermute | solution.py:20
  (70 shorter events, 42.6 us)
Async XLA Ops:
  7.2 399.1 %all-reduce.40.cloned.1.call-start = ((), (), s32[]{:S(2)}) async-start(), calls=%async_computation | async-start | bytes 1048576 | tf_op jit(solution)/shard_map/psum | solution.py:177
  7.2 0.7 copy-start.5
  9.1 15.9 %copy-start.3 = (s32[3,8192]{1,0:T(4,128)S(1)}, s32[3,8192]{1,0:T(4,128)}, u32[]{:S(2)}) copy-start(s32[3,8192]{1,0:T(4,128)} %param.7) | copy-start | bytes 294916
  10.4 17.0 %collective-permute-start.1 = (f32[1,1,512,256]{3,2,1,0:T(8,128)S(1)}, f32[1,1,512,256]{3,2,1,0:T(8,128)S(1)}, u32[]{:S(2)}, u32[]{:S(2)}) collective-permute-start(f32[1,1,512,256]{3,2,1,0:T(8,128)S(1)} %add_sqrt_fusion), channel_id=1, source_target_pairs={{1,0},{2,1},{3,2},{4,3},{5,4},{6,5},{7,6},{8,7},{9,8},{10,9},{11,1... | collective-permute-start | bytes 1572872 | tf_op jit(solution)/shard_map/ppermute | solution.py:21
  20.8 12.6 %collective-permute-start = (f32[1,1,512,256]{3,2,1,0:T(8,128)S(1)}, f32[1,1,512,256]{3,2,1,0:T(8,128)S(1)}, u32[]{:S(2)}, u32[]{:S(2)}) collective-permute-start(f32[1,1,512,256]{3,2,1,0:T(8,128)S(1)} %add_sqrt_fusion), channel_id=1, source_target_pairs={{0,1},{1,2},{2,3},{3,4},{4,5},{5,6},{6,7},{7,8},{8,9},{9,10},{10,1... | collective-permute-start | bytes 1572872 | tf_op jit(solution)/shard_map/ppermute | solution.py:20
  23.9 0.7 copy-start.6
  25.4 8.0 %copy-start.1 = (f32[1,512,256]{2,1,0:T(8,128)S(1)}, f32[1,512,256]{2,1,0:T(8,128)}, u32[]{:S(2)}) copy-start(f32[1,512,256]{2,1,0:T(8,128)} %param.5) | copy-start | bytes 1572868
  36.0 8.6 %collective-permute-start.3 = (f32[1,1,512,256]{3,2,1,0:T(8,128)S(1)}, f32[1,1,512,256]{3,2,1,0:T(8,128)S(1)}, u32[]{:S(2)}, u32[]{:S(2)}) collective-permute-start(f32[1,1,512,256]{3,2,1,0:T(8,128)S(1)} %fusion.1), channel_id=1, source_target_pairs={{1,0},{2,1},{3,2},{4,3},{5,4},{6,5},{7,6},{8,7},{9,8},{10,9},{11,1... | collective-permute-start | bytes 1572872 | tf_op jit(solution)/shard_map/ppermute | solution.py:21
  37.9 12.6 %collective-permute-start.2 = (f32[1,1,512,256]{3,2,1,0:T(8,128)S(1)}, f32[1,1,512,256]{3,2,1,0:T(8,128)S(1)}, u32[]{:S(2)}, u32[]{:S(2)}) collective-permute-start(f32[1,1,512,256]{3,2,1,0:T(8,128)S(1)} %fusion.1), channel_id=1, source_target_pairs={{0,1},{1,2},{2,3},{3,4},{4,5},{5,6},{6,7},{7,8},{8,9},{9,10},{10,1... | collective-permute-start | bytes 1572872 | tf_op jit(solution)/shard_map/ppermute | solution.py:20
  52.8 8.6 %collective-permute-start.5 = (f32[1,1,512,256]{3,2,1,0:T(8,128)S(1)}, f32[1,1,512,256]{3,2,1,0:T(8,128)S(1)}, u32[]{:S(2)}, u32[]{:S(2)}) collective-permute-start(f32[1,1,512,256]{3,2,1,0:T(8,128)S(1)} %fusion.3), channel_id=1, source_target_pairs={{1,0},{2,1},{3,2},{4,3},{5,4},{6,5},{7,6},{8,7},{9,8},{10,9},{11,1... | collective-permute-start | bytes 1572872 | tf_op jit(solution)/shard_map/ppermute | solution.py:21
  54.7 12.6 %collective-permute-start.4 = (f32[1,1,512,256]{3,2,1,0:T(8,128)S(1)}, f32[1,1,512,256]{3,2,1,0:T(8,128)S(1)}, u32[]{:S(2)}, u32[]{:S(2)}) collective-permute-start(f32[1,1,512,256]{3,2,1,0:T(8,128)S(1)} %fusion.3), channel_id=1, source_target_pairs={{0,1},{1,2},{2,3},{3,4},{4,5},{5,6},{6,7},{7,8},{8,9},{9,10},{10,1... | collective-permute-start | bytes 1572872 | tf_op jit(solution)/shard_map/ppermute | solution.py:20
  69.6 8.6 %collective-permute-start.7 = (f32[1,1,512,256]{3,2,1,0:T(8,128)S(1)}, f32[1,1,512,256]{3,2,1,0:T(8,128)S(1)}, u32[]{:S(2)}, u32[]{:S(2)}) collective-permute-start(f32[1,1,512,256]{3,2,1,0:T(8,128)S(1)} %fusion.5), channel_id=1, source_target_pairs={{1,0},{2,1},{3,2},{4,3},{5,4},{6,5},{7,6},{8,7},{9,8},{10,9},{11,1... | collective-permute-start | bytes 1572872 | tf_op jit(solution)/shard_map/ppermute | solution.py:21
  71.5 12.6 %collective-permute-start.6 = (f32[1,1,512,256]{3,2,1,0:T(8,128)S(1)}, f32[1,1,512,256]{3,2,1,0:T(8,128)S(1)}, u32[]{:S(2)}, u32[]{:S(2)}) collective-permute-start(f32[1,1,512,256]{3,2,1,0:T(8,128)S(1)} %fusion.5), channel_id=1, source_target_pairs={{0,1},{1,2},{2,3},{3,4},{4,5},{5,6},{6,7},{7,8},{8,9},{9,10},{10,1... | collective-permute-start | bytes 1572872 | tf_op jit(solution)/shard_map/ppermute | solution.py:20
  86.4 113.6 %copy-start = (f32[1,1,512,256]{3,2,1,0:T(8,128)}, f32[1,1,512,256]{3,2,1,0:T(8,128)S(1)}, u32[]{:S(2)}) copy-start(f32[1,1,512,256]{3,2,1,0:T(8,128)S(1)} %fusion.7) | copy-start | bytes 1572868
  86.7 45.6 %copy-start.4 = (f32[1,8192]{1,0:T(1,128)S(1)}, f32[1,8192]{1,0:T(1,128)}, u32[]{:S(2)}) copy-start(f32[1,8192]{1,0:T(1,128)} %param.8) | copy-start | bytes 98308
  177.8 12.3 %collective-permute-start.11 = (f32[1,1,512,256]{3,2,1,0:T(8,128)S(1)}, f32[1,1,512,256]{3,2,1,0:T(8,128)S(1)}, u32[]{:S(2)}, u32[]{:S(2)}) collective-permute-start(f32[1,1,512,256]{3,2,1,0:T(8,128)S(1)} %reshape.397), channel_id=1, source_target_pairs={{1,0},{2,1},{3,2},{4,3},{5,4},{6,5},{7,6},{8,7},{9,8},{10,9},{11,1... | collective-permute-start | bytes 1572872 | tf_op jit(solution)/shard_map/ppermute | solution.py:21
  179.8 12.6 %collective-permute-start.9 = (f32[1,1,512,256]{3,2,1,0:T(8,128)S(1)}, f32[1,1,512,256]{3,2,1,0:T(8,128)S(1)}, u32[]{:S(2)}, u32[]{:S(2)}) collective-permute-start(f32[1,1,512,256]{3,2,1,0:T(8,128)S(1)} %reshape.397), channel_id=1, source_target_pairs={{0,1},{1,2},{2,3},{3,4},{4,5},{5,6},{6,7},{7,8},{8,9},{9,10},{10,1... | collective-permute-start | bytes 1572872 | tf_op jit(solution)/shard_map/ppermute | solution.py:20
  182.2 12.0 %collective-permute-start.10 = (f32[1,1,512,256]{3,2,1,0:T(8,128)S(1)}, f32[1,1,512,256]{3,2,1,0:T(8,128)S(1)}, u32[]{:S(2)}, u32[]{:S(2)}) collective-permute-start(f32[1,1,512,256]{3,2,1,0:T(8,128)S(1)} %fusion.7), channel_id=1, source_target_pairs={{1,0},{2,1},{3,2},{4,3},{5,4},{6,5},{7,6},{8,7},{9,8},{10,9},{11,1... | collective-permute-start | bytes 1572872 | tf_op jit(solution)/shard_map/ppermute | solution.py:21
  187.4 12.6 %collective-permute-start.8 = (f32[1,1,512,256]{3,2,1,0:T(8,128)S(1)}, f32[1,1,512,256]{3,2,1,0:T(8,128)S(1)}, u32[]{:S(2)}, u32[]{:S(2)}) collective-permute-start(f32[1,1,512,256]{3,2,1,0:T(8,128)S(1)} %fusion.7), channel_id=1, source_target_pairs={{0,1},{1,2},{2,3},{3,4},{4,5},{5,6},{6,7},{7,8},{8,9},{9,10},{10,1... | collective-permute-start | bytes 1572872 | tf_op jit(solution)/shard_map/ppermute | solution.py:20
  201.0 8.6 %collective-permute-start.13 = (f32[1,1,512,256]{3,2,1,0:T(8,128)S(1)}, f32[1,1,512,256]{3,2,1,0:T(8,128)S(1)}, u32[]{:S(2)}, u32[]{:S(2)}) collective-permute-start(f32[1,1,512,256]{3,2,1,0:T(8,128)S(1)} %get-tuple-element.4), channel_id=1, source_target_pairs={{1,0},{2,1},{3,2},{4,3},{5,4},{6,5},{7,6},{8,7},{9,8},{10,9},{11,1... | collective-permute-start | bytes 1572872 | tf_op jit(solution)/shard_map/ppermute | solution.py:21
  202.9 12.6 %collective-permute-start.12 = (f32[1,1,512,256]{3,2,1,0:T(8,128)S(1)}, f32[1,1,512,256]{3,2,1,0:T(8,128)S(1)}, u32[]{:S(2)}, u32[]{:S(2)}) collective-permute-start(f32[1,1,512,256]{3,2,1,0:T(8,128)S(1)} %get-tuple-element.4), channel_id=1, source_target_pairs={{0,1},{1,2},{2,3},{3,4},{4,5},{5,6},{6,7},{7,8},{8,9},{9,10},{10,1... | collective-permute-start | bytes 1572872 | tf_op jit(solution)/shard_map/ppermute | solution.py:20
  216.0 8.6 %collective-permute-start.15 = (f32[1,1,512,256]{3,2,1,0:T(8,128)S(1)}, f32[1,1,512,256]{3,2,1,0:T(8,128)S(1)}, u32[]{:S(2)}, u32[]{:S(2)}) collective-permute-start(f32[1,1,512,256]{3,2,1,0:T(8,128)S(1)} %multiply_add_fusion.1), channel_id=1, source_target_pairs={{1,0},{2,1},{3,2},{4,3},{5,4},{6,5},{7,6},{8,7},{9,8},{10,9},{11,1... | collective-permute-start | bytes 1572872 | tf_op jit(solution)/shard_map/ppermute | solution.py:21
  217.9 12.6 %collective-permute-start.14 = (f32[1,1,512,256]{3,2,1,0:T(8,128)S(1)}, f32[1,1,512,256]{3,2,1,0:T(8,128)S(1)}, u32[]{:S(2)}, u32[]{:S(2)}) collective-permute-start(f32[1,1,512,256]{3,2,1,0:T(8,128)S(1)} %multiply_add_fusion.1), channel_id=1, source_target_pairs={{0,1},{1,2},{2,3},{3,4},{4,5},{5,6},{6,7},{7,8},{8,9},{9,10},{10,1... | collective-permute-start | bytes 1572872 | tf_op jit(solution)/shard_map/ppermute | solution.py:20
  231.0 8.6 %collective-permute-start.17 = (f32[1,1,512,256]{3,2,1,0:T(8,128)S(1)}, f32[1,1,512,256]{3,2,1,0:T(8,128)S(1)}, u32[]{:S(2)}, u32[]{:S(2)}) collective-permute-start(f32[1,1,512,256]{3,2,1,0:T(8,128)S(1)} %multiply_add_fusion), channel_id=1, source_target_pairs={{1,0},{2,1},{3,2},{4,3},{5,4},{6,5},{7,6},{8,7},{9,8},{10,9},{11,1... | collective-permute-start | bytes 1572872 | tf_op jit(solution)/shard_map/ppermute | solution.py:21
  232.9 12.6 %collective-permute-start.16 = (f32[1,1,512,256]{3,2,1,0:T(8,128)S(1)}, f32[1,1,512,256]{3,2,1,0:T(8,128)S(1)}, u32[]{:S(2)}, u32[]{:S(2)}) collective-permute-start(f32[1,1,512,256]{3,2,1,0:T(8,128)S(1)} %multiply_add_fusion), channel_id=1, source_target_pairs={{0,1},{1,2},{2,3},{3,4},{4,5},{5,6},{6,7},{7,8},{8,9},{9,10},{10,1... | collective-permute-start | bytes 1572872 | tf_op jit(solution)/shard_map/ppermute | solution.py:20
  406.2 8.9 %collective-permute-start.19 = (f32[1,512,256]{2,1,0:T(8,128)}, f32[1,512,256]{2,1,0:T(8,128)S(1)}, u32[]{:S(2)}, u32[]{:S(2)}) collective-permute-start(f32[1,512,256]{2,1,0:T(8,128)} %all-reduce.40.cloned.1.call-done), channel_id=1, source_target_pairs={{1,0},{2,1},{3,2},{4,3},{5,4},{6,5},{7,6},{8,7},{9,8},{10,9},{11,1... | collective-permute-start | bytes 1572872 | tf_op jit(solution)/shard_map/ppermute | solution.py:21
  408.2 13.5 %collective-permute-start.18 = (f32[1,512,256]{2,1,0:T(8,128)}, f32[1,512,256]{2,1,0:T(8,128)S(1)}, u32[]{:S(2)}, u32[]{:S(2)}) collective-permute-start(f32[1,512,256]{2,1,0:T(8,128)} %all-reduce.40.cloned.1.call-done), channel_id=1, source_target_pairs={{0,1},{1,2},{2,3},{3,4},{4,5},{5,6},{6,7},{7,8},{8,9},{9,10},{10,1... | collective-permute-start | bytes 1572872 | tf_op jit(solution)/shard_map/ppermute | solution.py:20
  410.6 12.2 %copy-start.2 = (f32[1,512,256]{2,1,0:T(8,128)S(1)}, f32[1,512,256]{2,1,0:T(8,128)}, u32[]{:S(2)}) copy-start(f32[1,512,256]{2,1,0:T(8,128)} %all-reduce.40.cloned.1.call-done) | copy-start | bytes 1572868
Sparse Core Ops, SparseCore 0:
  247.1 159.1 all-reduce.39
where the time goes:
time: 432 us; the launch traced here: 431 us
  waiting for transfers between devices  248 us (57%)
  other arithmetic  62.1 us (14%)
  starting transfers between devices  54.3 us (13%)
  local copies, waits for them, and re-layouts  51.1 us (12%)
  between operations  15.7 us (4%)
    psum x1, waiting for transfers between devices, per_device(): summed_density = lax.psum(density, 'src')  159 us
    ppermute x10, waiting for transfers between devices, padded(): before = lax.ppermute(last, axis, up)  56.2 us
    gather x1, local copies, waits for them, and re-layouts, per_device(): jnp.take(flat_times, jnp.minimum(flat_index, cell_count - 1), axis=1)  45.5 us
    scatter-add x1, other arithmetic, per_device(): source = jnp.zeros((station_count, cell_count), jnp.float32).at[:, flat_i...  43.3 us
    ppermute x10, waiting for transfers between devices, padded(): after = lax.ppermute(first, axis, down)  32.1 us
    ppermute x10, starting transfers between devices, padded(): after = lax.ppermute(first, axis, down)  31 us
    ppermute x10, starting transfers between devices, padded(): before = lax.ppermute(last, axis, up)  23.3 us
    select_n x4, other arithmetic, sweep_once(): return jnp.where(station_mask, 0.0, chosen)  9.37 us
  transfers between devices with their start and end apart: 21, of which 20 were waited for; matrix products, arithmetic and copies ran while one was open for 1% of the time, Pallas kernels for 0%

commit v1 on v0

--- a/solution.py
+++ b/solution.py
@@ -174,7 +174,7 @@
             summed = summed + weight * neighbour
         adjoint = summed
     density = slowness * jnp.sum(adjoint, axis=0)
-    summed_density = lax.psum(density, "src")
+    summed_density = jnp.sum(lax.all_gather(density, "src"), axis=0)
     extended = padded(summed_density, (("space", 0),), 1)
     along_x = smooth_along(extended, 0)
     along_y = smooth_along(pad_zero(along_x, 1), 1)

time: 432 us -> 417 us (0.965)
  waiting for transfers between devices: 248 us -> 223 us
  other arithmetic: 62.1 us -> 69 us
    psum x1 -> x0, waiting for transfers between devices: 159 us -> none  [per_device(): summed_density = lax.psum(density, 'src')]
    all_gather x0 -> x1, waiting for transfers between devices: none -> 136 us  [per_device(): summed_density = jnp.sum(lax.all_gather(density, 'src'), axis=0)]
where the time goes in v1:
time: 417 us; the launch traced here: 416 us
  waiting for transfers between devices  223 us (53%)
  other arithmetic  69 us (17%)
  starting transfers between devices  57.7 us (14%)
  local copies, waits for them, and re-layouts  50.6 us (12%)
  between operations  15.7 us (4%)
    all_gather x1, waiting for transfers between devices, per_device(): summed_density = jnp.sum(lax.all_gather(density, 'src'), axis=0)  136 us
    ppermute x10, waiting for transfers between devices, padded(): before = lax.ppermute(last, axis, up)  55.7 us
    gather x1, local copies, waits for them, and re-layouts, per_device(): jnp.take(flat_times, jnp.minimum(flat_index, cell_count - 1), axis=1)  45.5 us
    scatter-add x1, other arithmetic, per_device(): source = jnp.zeros((station_count, cell_count), jnp.float32).at[:, flat_i...  43.3 us
    ppermute x10, starting transfers between devices, padded(): after = lax.ppermute(first, axis, down)  34.9 us
    ppermute x10, waiting for transfers between devices, padded(): after = lax.ppermute(first, axis, down)  31.2 us
    ppermute x10, starting transfers between devices, padded(): before = lax.ppermute(last, axis, up)  22.8 us
    select_n x4, other arithmetic, sweep_once(): return jnp.where(station_mask, 0.0, chosen)  11.1 us
  transfers between devices with their start and end apart: 21, of which 20 were waited for; matrix products, arithmetic and copies ran while one was open for 1% of the time, Pallas kernels for 0%

profile of v1, /device:TPU:2, one launch (start us, length us, event | category | flops | bytes accessed | tf_op | source)
XLA Modules:
  0.0 416.1 jit_solution(12712590173180804763)
XLA Ops:
  10.8 10.4 %collective-permute-start.1 = (f32[1,1,512,256]{3,2,1,0:T(8,128)S(1)}, f32[1,1,512,256]{3,2,1,0:T(8,128)S(1)}, u32[]{:S(2)}, u32[]{:S(2)}) collective-permute-start(f32[1,1,512,256]{3,2,1,0:T(8,128)S(1)} %add_sqrt_fusion), channel_id=1, source_target_pairs={{1,0},{2,1},{3,2},{4,3},{5,4},{6,5},{7,6},{8,7},{9,8},{10,9},{11,1... | collective-permute-start | bytes 1572872 | tf_op jit(solution)/shard_map/ppermute | solution.py:21
  27.8 5.9 %collective-permute-done = f32[1,1,512,256]{3,2,1,0:T(8,128)S(1)} collective-permute-done((f32[1,1,512,256]{3,2,1,0:T(8,128)S(1)}, f32[1,1,512,256]{3,2,1,0:T(8,128)S(1)}, u32[]{:S(2)}, u32[]{:S(2)}) %collective-permute-start) | collective-permute-done | bytes 524320 | tf_op jit(solution)/shard_map/ppermute | solution.py:20
  33.7 3.7 fusion.1
  39.3 2.4 collective-permute-start.2
  42.0 4.0 collective-permute-done.3
  46.0 5.9 %collective-permute-done.2 = f32[1,1,512,256]{3,2,1,0:T(8,128)S(1)} collective-permute-done((f32[1,1,512,256]{3,2,1,0:T(8,128)S(1)}, f32[1,1,512,256]{3,2,1,0:T(8,128)S(1)}, u32[]{:S(2)}, u32[]{:S(2)}) %collective-permute-start.2) | collective-permute-done | bytes 524320 | tf_op jit(solution)/shard_map/ppermute | solution.py:20
  51.9 2.5 fusion.3
  56.3 2.4 collective-permute-start.4
  59.0 4.0 collective-permute-done.5
  63.0 5.9 %collective-permute-done.4 = f32[1,1,512,256]{3,2,1,0:T(8,128)S(1)} collective-permute-done((f32[1,1,512,256]{3,2,1,0:T(8,128)S(1)}, f32[1,1,512,256]{3,2,1,0:T(8,128)S(1)}, u32[]{:S(2)}, u32[]{:S(2)}) %collective-permute-start.4) | collective-permute-done | bytes 524320 | tf_op jit(solution)/shard_map/ppermute | solution.py:20
  69.0 2.5 fusion.5
  73.4 2.4 collective-permute-start.6
  76.1 4.0 collective-permute-done.7
  80.0 5.9 %collective-permute-done.6 = f32[1,1,512,256]{3,2,1,0:T(8,128)S(1)} collective-permute-done((f32[1,1,512,256]{3,2,1,0:T(8,128)S(1)}, f32[1,1,512,256]{3,2,1,0:T(8,128)S(1)}, u32[]{:S(2)}, u32[]{:S(2)}) %collective-permute-start.6) | collective-permute-done | bytes 524320 | tf_op jit(solution)/shard_map/ppermute | solution.py:20
  86.0 2.5 fusion.7
  88.8 45.5 %gather_fusion = f32[8192]{0:T(1024)S(1)} fusion(f32[131072]{0:T(1024)S(1)} %bitcast.86, s32[8192]{0:T(1024)S(1)} %broadcast_clamp_fusion), kind=kCustom, calls=%fused_computation | custom fusion | bytes 98304 | tf_op jit(solution)/shard_map/jit(_take)/gather | solution.py:150
  136.6 43.3 %scatter_custom_fusion = f32[131072]{0:T(1024)S(1)} fusion(s32[8192]{0:T(1024)S(1)} %bitcast.93, f32[8192]{0:T(1024)S(1)} %bitcast.92, f32[]{:T(128)} %constant.24.clone.1), kind=kCustom, calls=%fused_computation.66 | custom fusion | flops 8192 | bytes 524292 | tf_op jit(solution)/shard_map/scatter-add | solution.py:159
  182.0 2.4 collective-permute-start.9
  184.4 5.3 %collective-permute-start.10 = (f32[1,1,512,256]{3,2,1,0:T(8,128)S(1)}, f32[1,1,512,256]{3,2,1,0:T(8,128)S(1)}, u32[]{:S(2)}, u32[]{:S(2)}) collective-permute-start(f32[1,1,512,256]{3,2,1,0:T(8,128)S(1)} %fusion.7), channel_id=1, source_target_pairs={{1,0},{2,1},{3,2},{4,3},{5,4},{6,5},{7,6},{8,7},{9,8},{10,9},{11,1... | collective-permute-start | bytes 1572872 | tf_op jit(solution)/shard_map/ppermute | solution.py:21
  196.4 5.9 %collective-permute-done.8 = f32[1,1,512,256]{3,2,1,0:T(8,128)S(1)} collective-permute-done((f32[1,1,512,256]{3,2,1,0:T(8,128)S(1)}, f32[1,1,512,256]{3,2,1,0:T(8,128)S(1)}, u32[]{:S(2)}, u32[]{:S(2)}) %collective-permute-start.8) | collective-permute-done | bytes 524320 | tf_op jit(solution)/shard_map/ppermute | solution.py:20
  205.1 2.4 collective-permute-start.12
  207.8 4.0 collective-permute-done.13
  211.8 5.9 %collective-permute-done.12 = f32[1,1,512,256]{3,2,1,0:T(8,128)S(1)} collective-permute-done((f32[1,1,512,256]{3,2,1,0:T(8,128)S(1)}, f32[1,1,512,256]{3,2,1,0:T(8,128)S(1)}, u32[]{:S(2)}, u32[]{:S(2)}) %collective-permute-start.12) | collective-permute-done | bytes 524320 | tf_op jit(solution)/shard_map/ppermute | solution.py:20
  222.9 4.0 collective-permute-done.15
  226.8 5.9 %collective-permute-done.14 = f32[1,1,512,256]{3,2,1,0:T(8,128)S(1)} collective-permute-done((f32[1,1,512,256]{3,2,1,0:T(8,128)S(1)}, f32[1,1,512,256]{3,2,1,0:T(8,128)S(1)}, u32[]{:S(2)}, u32[]{:S(2)}) %collective-permute-start.14) | collective-permute-done | bytes 524320 | tf_op jit(solution)/shard_map/ppermute | solution.py:20
  237.9 4.0 collective-permute-done.17
  241.9 5.9 %collective-permute-done.16 = f32[1,1,512,256]{3,2,1,0:T(8,128)S(1)} collective-permute-done((f32[1,1,512,256]{3,2,1,0:T(8,128)S(1)}, f32[1,1,512,256]{3,2,1,0:T(8,128)S(1)}, u32[]{:S(2)}, u32[]{:S(2)}) %collective-permute-start.16) | collective-permute-done | bytes 524320 | tf_op jit(solution)/shard_map/ppermute | solution.py:20
  249.4 136.2 %all-gather.3.cloned.1.call-done = f32[16,512,256]{2,1,0:T(8,128)} async-done(((f32[1,512,256]{2,1,0:T(8,128)}), f32[16,512,256]{2,1,0:T(8,128)}) %all-gather.3.cloned.1.call-update) | async-done | bytes 8388624 | tf_op jit(solution)/shard_map/all_gather | solution.py:177
  385.5 4.0 reduce.1
  389.5 5.8 %collective-permute-start.19 = (f32[1,512,256]{2,1,0:T(8,128)S(1)}, f32[1,512,256]{2,1,0:T(8,128)S(1)}, u32[]{:S(2)}, u32[]{:S(2)}) collective-permute-start(f32[1,512,256]{2,1,0:T(8,128)S(1)} %bitcast.88), channel_id=1, source_target_pairs={{1,0},{2,1},{3,2},{4,3},{5,4},{6,5},{7,6},{8,7},{9,8},{10,9},{11,1... | collective-permute-start | bytes 1572872 | tf_op jit(solution)/shard_map/ppermute | solution.py:21
  397.3 4.7 %collective-permute-done.19 = f32[1,512,256]{2,1,0:T(8,128)S(1)} collective-permute-done((f32[1,512,256]{2,1,0:T(8,128)S(1)}, f32[1,512,256]{2,1,0:T(8,128)S(1)}, u32[]{:S(2)}, u32[]{:S(2)}) %collective-permute-start.19) | collective-permute-done | bytes 524320 | tf_op jit(solution)/shard_map/ppermute | solution.py:21
  402.0 5.9 %collective-permute-done.18 = f32[1,512,256]{2,1,0:T(8,128)S(1)} collective-permute-done((f32[1,512,256]{2,1,0:T(8,128)S(1)}, f32[1,512,256]{2,1,0:T(8,128)S(1)}, u32[]{:S(2)}, u32[]{:S(2)}) %collective-permute-start.18) | collective-permute-done | bytes 524320 | tf_op jit(solution)/shard_map/ppermute | solution.py:20
  (65 shorter events, 44.8 us)
Async XLA Ops:
  7.2 44.8 %copy-start.1 = (f32[1,512,256]{2,1,0:T(8,128)S(1)}, f32[1,512,256]{2,1,0:T(8,128)}, u32[]{:S(2)}) copy-start(f32[1,512,256]{2,1,0:T(8,128)} %param.5) | copy-start | bytes 1572868
  7.2 378.4 %all-gather.3.cloned.1.call-start = ((), (), s32[]{:S(2)}) async-start(), calls=%async_computation | async-start | bytes 8912896 | tf_op jit(solution)/shard_map/all_gather | solution.py:177
  10.8 17.0 %collective-permute-start.1 = (f32[1,1,512,256]{3,2,1,0:T(8,128)S(1)}, f32[1,1,512,256]{3,2,1,0:T(8,128)S(1)}, u32[]{:S(2)}, u32[]{:S(2)}) collective-permute-start(f32[1,1,512,256]{3,2,1,0:T(8,128)S(1)} %add_sqrt_fusion), channel_id=1, source_target_pairs={{1,0},{2,1},{3,2},{4,3},{5,4},{6,5},{7,6},{8,7},{9,8},{10,9},{11,1... | collective-permute-start | bytes 1572872 | tf_op jit(solution)/shard_map/ppermute | solution.py:21
  21.1 12.6 %collective-permute-start = (f32[1,1,512,256]{3,2,1,0:T(8,128)S(1)}, f32[1,1,512,256]{3,2,1,0:T(8,128)S(1)}, u32[]{:S(2)}, u32[]{:S(2)}) collective-permute-start(f32[1,1,512,256]{3,2,1,0:T(8,128)S(1)} %add_sqrt_fusion), channel_id=1, source_target_pairs={{0,1},{1,2},{2,3},{3,4},{4,5},{5,6},{6,7},{7,8},{8,9},{9,10},{10,1... | collective-permute-start | bytes 1572872 | tf_op jit(solution)/shard_map/ppermute | solution.py:20
  37.4 8.6 %collective-permute-start.3 = (f32[1,1,512,256]{3,2,1,0:T(8,128)S(1)}, f32[1,1,512,256]{3,2,1,0:T(8,128)S(1)}, u32[]{:S(2)}, u32[]{:S(2)}) collective-permute-start(f32[1,1,512,256]{3,2,1,0:T(8,128)S(1)} %fusion.1), channel_id=1, source_target_pairs={{1,0},{2,1},{3,2},{4,3},{5,4},{6,5},{7,6},{8,7},{9,8},{10,9},{11,1... | collective-permute-start | bytes 1572872 | tf_op jit(solution)/shard_map/ppermute | solution.py:21
  39.3 12.6 %collective-permute-start.2 = (f32[1,1,512,256]{3,2,1,0:T(8,128)S(1)}, f32[1,1,512,256]{3,2,1,0:T(8,128)S(1)}, u32[]{:S(2)}, u32[]{:S(2)}) collective-permute-start(f32[1,1,512,256]{3,2,1,0:T(8,128)S(1)} %fusion.1), channel_id=1, source_target_pairs={{0,1},{1,2},{2,3},{3,4},{4,5},{5,6},{6,7},{7,8},{8,9},{9,10},{10,1... | collective-permute-start | bytes 1572872 | tf_op jit(solution)/shard_map/ppermute | solution.py:20
  54.4 8.6 %collective-permute-start.5 = (f32[1,1,512,256]{3,2,1,0:T(8,128)S(1)}, f32[1,1,512,256]{3,2,1,0:T(8,128)S(1)}, u32[]{:S(2)}, u32[]{:S(2)}) collective-permute-start(f32[1,1,512,256]{3,2,1,0:T(8,128)S(1)} %fusion.3), channel_id=1, source_target_pairs={{1,0},{2,1},{3,2},{4,3},{5,4},{6,5},{7,6},{8,7},{9,8},{10,9},{11,1... | collective-permute-start | bytes 1572872 | tf_op jit(solution)/shard_map/ppermute | solution.py:21
  56.3 12.6 %collective-permute-start.4 = (f32[1,1,512,256]{3,2,1,0:T(8,128)S(1)}, f32[1,1,512,256]{3,2,1,0:T(8,128)S(1)}, u32[]{:S(2)}, u32[]{:S(2)}) collective-permute-start(f32[1,1,512,256]{3,2,1,0:T(8,128)S(1)} %fusion.3), channel_id=1, source_target_pairs={{0,1},{1,2},{2,3},{3,4},{4,5},{5,6},{6,7},{7,8},{8,9},{9,10},{10,1... | collective-permute-start | bytes 1572872 | tf_op jit(solution)/shard_map/ppermute | solution.py:20
  71.4 8.6 %collective-permute-start.7 = (f32[1,1,512,256]{3,2,1,0:T(8,128)S(1)}, f32[1,1,512,256]{3,2,1,0:T(8,128)S(1)}, u32[]{:S(2)}, u32[]{:S(2)}) collective-permute-start(f32[1,1,512,256]{3,2,1,0:T(8,128)S(1)} %fusion.5), channel_id=1, source_target_pairs={{1,0},{2,1},{3,2},{4,3},{5,4},{6,5},{7,6},{8,7},{9,8},{10,9},{11,1... | collective-permute-start | bytes 1572872 | tf_op jit(solution)/shard_map/ppermute | solution.py:21
  73.4 12.6 %collective-permute-start.6 = (f32[1,1,512,256]{3,2,1,0:T(8,128)S(1)}, f32[1,1,512,256]{3,2,1,0:T(8,128)S(1)}, u32[]{:S(2)}, u32[]{:S(2)}) collective-permute-start(f32[1,1,512,256]{3,2,1,0:T(8,128)S(1)} %fusion.5), channel_id=1, source_target_pairs={{0,1},{1,2},{2,3},{3,4},{4,5},{5,6},{6,7},{7,8},{8,9},{9,10},{10,1... | collective-permute-start | bytes 1572872 | tf_op jit(solution)/shard_map/ppermute | solution.py:20
  88.4 113.9 %copy-start = (f32[1,1,512,256]{3,2,1,0:T(8,128)}, f32[1,1,512,256]{3,2,1,0:T(8,128)S(1)}, u32[]{:S(2)}) copy-start(f32[1,1,512,256]{3,2,1,0:T(8,128)S(1)} %fusion.7) | copy-start | bytes 1572868
  88.7 45.6 %copy-start.2 = (s32[3,8192]{1,0:T(4,128)S(1)}, s32[3,8192]{1,0:T(4,128)}, u32[]{:S(2)}) copy-start(s32[3,8192]{1,0:T(4,128)} %param.7) | copy-start | bytes 294916
  88.8 45.6 %copy-start.3 = (f32[1,8192]{1,0:T(1,128)S(1)}, f32[1,8192]{1,0:T(1,128)}, u32[]{:S(2)}) copy-start(f32[1,8192]{1,0:T(1,128)} %param.8) | copy-start | bytes 98308
  180.1 12.3 %collective-permute-start.11 = (f32[1,1,512,256]{3,2,1,0:T(8,128)S(1)}, f32[1,1,512,256]{3,2,1,0:T(8,128)S(1)}, u32[]{:S(2)}, u32[]{:S(2)}) collective-permute-start(f32[1,1,512,256]{3,2,1,0:T(8,128)S(1)} %reshape.406), channel_id=1, source_target_pairs={{1,0},{2,1},{3,2},{4,3},{5,4},{6,5},{7,6},{8,7},{9,8},{10,9},{11,1... | collective-permute-start | bytes 1572872 | tf_op jit(solution)/shard_map/ppermute | solution.py:21
  182.0 12.6 %collective-permute-start.9 = (f32[1,1,512,256]{3,2,1,0:T(8,128)S(1)}, f32[1,1,512,256]{3,2,1,0:T(8,128)S(1)}, u32[]{:S(2)}, u32[]{:S(2)}) collective-permute-start(f32[1,1,512,256]{3,2,1,0:T(8,128)S(1)} %reshape.406), channel_id=1, source_target_pairs={{0,1},{1,2},{2,3},{3,4},{4,5},{5,6},{6,7},{7,8},{8,9},{9,10},{10,1... | collective-permute-start | bytes 1572872 | tf_op jit(solution)/shard_map/ppermute | solution.py:20
  184.4 12.0 %collective-permute-start.10 = (f32[1,1,512,256]{3,2,1,0:T(8,128)S(1)}, f32[1,1,512,256]{3,2,1,0:T(8,128)S(1)}, u32[]{:S(2)}, u32[]{:S(2)}) collective-permute-start(f32[1,1,512,256]{3,2,1,0:T(8,128)S(1)} %fusion.7), channel_id=1, source_target_pairs={{1,0},{2,1},{3,2},{4,3},{5,4},{6,5},{7,6},{8,7},{9,8},{10,9},{11,1... | collective-permute-start | bytes 1572872 | tf_op jit(solution)/shard_map/ppermute | solution.py:21
  189.7 12.6 %collective-permute-start.8 = (f32[1,1,512,256]{3,2,1,0:T(8,128)S(1)}, f32[1,1,512,256]{3,2,1,0:T(8,128)S(1)}, u32[]{:S(2)}, u32[]{:S(2)}) collective-permute-start(f32[1,1,512,256]{3,2,1,0:T(8,128)S(1)} %fusion.7), channel_id=1, source_target_pairs={{0,1},{1,2},{2,3},{3,4},{4,5},{5,6},{6,7},{7,8},{8,9},{9,10},{10,1... | collective-permute-start | bytes 1572872 | tf_op jit(solution)/shard_map/ppermute | solution.py:20
  203.2 8.6 %collective-permute-start.13 = (f32[1,1,512,256]{3,2,1,0:T(8,128)S(1)}, f32[1,1,512,256]{3,2,1,0:T(8,128)S(1)}, u32[]{:S(2)}, u32[]{:S(2)}) collective-permute-start(f32[1,1,512,256]{3,2,1,0:T(8,128)S(1)} %get-tuple-element.4), channel_id=1, source_target_pairs={{1,0},{2,1},{3,2},{4,3},{5,4},{6,5},{7,6},{8,7},{9,8},{10,9},{11,1... | collective-permute-start | bytes 1572872 | tf_op jit(solution)/shard_map/ppermute | solution.py:21
  205.1 12.6 %collective-permute-start.12 = (f32[1,1,512,256]{3,2,1,0:T(8,128)S(1)}, f32[1,1,512,256]{3,2,1,0:T(8,128)S(1)}, u32[]{:S(2)}, u32[]{:S(2)}) collective-permute-start(f32[1,1,512,256]{3,2,1,0:T(8,128)S(1)} %get-tuple-element.4), channel_id=1, source_target_pairs={{0,1},{1,2},{2,3},{3,4},{4,5},{5,6},{6,7},{7,8},{8,9},{9,10},{10,1... | collective-permute-start | bytes 1572872 | tf_op jit(solution)/shard_map/ppermute | solution.py:20
  218.2 8.6 %collective-permute-start.15 = (f32[1,1,512,256]{3,2,1,0:T(8,128)S(1)}, f32[1,1,512,256]{3,2,1,0:T(8,128)S(1)}, u32[]{:S(2)}, u32[]{:S(2)}) collective-permute-start(f32[1,1,512,256]{3,2,1,0:T(8,128)S(1)} %multiply_add_fusion.1), channel_id=1, source_target_pairs={{1,0},{2,1},{3,2},{4,3},{5,4},{6,5},{7,6},{8,7},{9,8},{10,9},{11,1... | collective-permute-start | bytes 1572872 | tf_op jit(solution)/shard_map/ppermute | solution.py:21
  220.2 12.6 %collective-permute-start.14 = (f32[1,1,512,256]{3,2,1,0:T(8,128)S(1)}, f32[1,1,512,256]{3,2,1,0:T(8,128)S(1)}, u32[]{:S(2)}, u32[]{:S(2)}) collective-permute-start(f32[1,1,512,256]{3,2,1,0:T(8,128)S(1)} %multiply_add_fusion.1), channel_id=1, source_target_pairs={{0,1},{1,2},{2,3},{3,4},{4,5},{5,6},{6,7},{7,8},{8,9},{9,10},{10,1... | collective-permute-start | bytes 1572872 | tf_op jit(solution)/shard_map/ppermute | solution.py:20
  233.3 8.6 %collective-permute-start.17 = (f32[1,1,512,256]{3,2,1,0:T(8,128)S(1)}, f32[1,1,512,256]{3,2,1,0:T(8,128)S(1)}, u32[]{:S(2)}, u32[]{:S(2)}) collective-permute-start(f32[1,1,512,256]{3,2,1,0:T(8,128)S(1)} %multiply_add_fusion), channel_id=1, source_target_pairs={{1,0},{2,1},{3,2},{4,3},{5,4},{6,5},{7,6},{8,7},{9,8},{10,9},{11,1... | collective-permute-start | bytes 1572872 | tf_op jit(solution)/shard_map/ppermute | solution.py:21
  235.2 12.6 %collective-permute-start.16 = (f32[1,1,512,256]{3,2,1,0:T(8,128)S(1)}, f32[1,1,512,256]{3,2,1,0:T(8,128)S(1)}, u32[]{:S(2)}, u32[]{:S(2)}) collective-permute-start(f32[1,1,512,256]{3,2,1,0:T(8,128)S(1)} %multiply_add_fusion), channel_id=1, source_target_pairs={{0,1},{1,2},{2,3},{3,4},{4,5},{5,6},{6,7},{7,8},{8,9},{9,10},{10,1... | collective-permute-start | bytes 1572872 | tf_op jit(solution)/shard_map/ppermute | solution.py:20
  389.5 12.5 %collective-permute-start.19 = (f32[1,512,256]{2,1,0:T(8,128)S(1)}, f32[1,512,256]{2,1,0:T(8,128)S(1)}, u32[]{:S(2)}, u32[]{:S(2)}) collective-permute-start(f32[1,512,256]{2,1,0:T(8,128)S(1)} %bitcast.88), channel_id=1, source_target_pairs={{1,0},{2,1},{3,2},{4,3},{5,4},{6,5},{7,6},{8,7},{9,8},{10,9},{11,1... | collective-permute-start | bytes 1572872 | tf_op jit(solution)/shard_map/ppermute | solution.py:21
  395.3 12.6 %collective-permute-start.18 = (f32[1,512,256]{2,1,0:T(8,128)S(1)}, f32[1,512,256]{2,1,0:T(8,128)S(1)}, u32[]{:S(2)}, u32[]{:S(2)}) collective-permute-start(f32[1,512,256]{2,1,0:T(8,128)S(1)} %bitcast.89), channel_id=1, source_target_pairs={{0,1},{1,2},{2,3},{3,4},{4,5},{5,6},{6,7},{7,8},{8,9},{9,10},{10,1... | collective-permute-start | bytes 1572872 | tf_op jit(solution)/shard_map/ppermute | solution.py:20
Sparse Core Ops, SparseCore 0:
  249.5 136.0 all-gather.2
